TPU v7x, 256 devices: a whole 4x4x8 slice. The times are simulated.
256 devices in a mesh: layer: 32 (over x, z), box: 8 (over y, core).
Axes of the slice: x: 4, y: 4, z: 8, core: 2. Of those that a mesh axis runs over, the one named last changes fastest.
Arguments:
- box_maps: bfloat16 [32, 8192, 1024], P('layer', 'box'), may hold values from -0.1875 to 0.1875
- block_pattern: int32 [32, 64, 8], P('layer', 'box'), may hold values 0 or 1
- face_inverses: float32 [32, 7, 256, 256], P('layer'), may hold values from -0.375 to 0.375
- index_map: int32 [32, 1024], P('layer'), may hold values from 0 to 1023, each once within a row
- sources: float32 [32, 16, 1024], P('layer', 'box'), may hold values from -2.5 to 2.5
Outputs:
- merged: bfloat16 [32, 1024, 1024], P('layer')
- sweep_trace: float32 [32, 16, 1024], P('layer', 'box')
Inputs may be any that keep to these rules, and one draw needn't show every extreme that they name: Each row of index_map is a permutation of 0 to 1023.
All inputs are finite; a program needn't handle non-finite values. No bound on the sum of `block_pattern` on one device may be relied on, other than what follows from the above.
Results may differ from a plain program's by a relative error of at most 0.025.
Values may be sent and summed in bfloat16 or wider, within the bound.
A program may use at most 64 MiB of HBM per device.

v0:
```python
import jax
import jax.numpy as jnp
from jax import lax
from jax.sharding import PartitionSpec as P


def partner_2(value, axis, distance):
    mask = 2**distance
    pairs = [(source, source ^ mask) for source in range(lax.axis_size(axis))]
    return lax.ppermute(value, axis, pairs)


def shifted(block, axis, distance):
    devices = range(lax.axis_size(axis))
    route = [(i - distance, i) for i in devices if i - distance in devices]
    return lax.ppermute(block, axis, route)


def mask_map(one_map, one_pattern):
    blocks_count = one_pattern.shape[0]
    width = one_map.shape[0]
    tiles = one_map.reshape(
        blocks_count, width // blocks_count, blocks_count, width // blocks_count
    )
    kept = one_pattern.astype(jnp.bfloat16)[:, None, :, None]
    return (tiles * kept).reshape(width, width)


def combine(first, second, inverse, level):
    face_size = inverse.shape[0]
    joined = 0.5 * (first.astype(jnp.float32) + second.astype(jnp.float32))
    left_cols = joined[:, level * face_size : (level + 1) * face_size]
    right_rows = joined[level * face_size : (level + 1) * face_size, :]
    product = jnp.dot(left_cols, inverse, precision=lax.Precision.HIGHEST)
    return (joined - jnp.dot(product, right_rows, precision=lax.Precision.HIGHEST)).astype(
        jnp.bfloat16
    )


def on_device(box_maps, block_pattern, face_inverses, index_map, sources):
    boxes = lax.axis_size("box")
    layers = lax.axis_size("layer")
    coupling = float(boxes) ** 0.5
    levels = boxes.bit_length() - 1
    leaf = mask_map(box_maps[0], block_pattern[0])
    inverses = face_inverses[0]
    current = leaf
    position = lax.axis_index("box")
    for level in range(levels):
        partner = partner_2(current, "box", level)
        tree_node = (boxes >> level + 1) - 1 + (position >> level + 1)
        chosen = lax.dynamic_index_in_dim(inverses, tree_node, 0, keepdims=False)
        current = combine(current, partner, chosen, level)
    merged = current
    source_rows = sources[0]
    order_map = index_map[0]
    initial = jnp.zeros(source_rows.shape, jnp.float32)

    def down_step(step, state):
        received = shifted(state, "layer", 1)
        gathered = received[:, order_map].astype(jnp.bfloat16)
        return source_rows + coupling * jnp.dot(
            gathered, merged.T, preferred_element_type=jnp.float32
        )

    downward = lax.fori_loop(0, layers, down_step, initial)

    def up_step(step, state):
        received = shifted(state, "layer", -1)
        return downward + coupling * jnp.dot(
            received.astype(jnp.bfloat16), merged, preferred_element_type=jnp.float32
        )

    upward = lax.fori_loop(0, layers, up_step, initial)
    return (merged[None], upward[None])


def solution(mesh):
    return jax.shard_map(
        on_device,
        mesh=mesh,
        in_specs=(
            P("layer", "box", None),
            P("layer", "box", None),
            P("layer", None, None, None),
            P("layer", None),
            P("layer", "box", None),
        ),
        out_specs=(P("layer", None, None), P("layer", "box", None)),
        check_vma=False,
    )
```

profile of v0, /device:TPU:6, one launch (start us, length us, event | category | flops | bytes accessed | tf_op | source)
XLA Modules:
  0.0 863.7 jit_solution(3729378394479106907)
XLA Ops:
  20.0 46.4 %collective-permute-done.3 = bf16[1024,1024]{1,0:T(8,128)(2,1)} collective-permute-done((bf16[1024,1024]{1,0:T(8,128)(2,1)}, bf16[1024,1024]{1,0:T(8,128)(2,1)}, u32[]{:S(2)}, u32[]{:S(2)}) %collective-permute-start.3) | collective-permute-done | bytes 2097184 | tf_op jit(solution)/shard_map/ppermute | solution.py:10
  78.4 45.4 %collective-permute-done.4 = bf16[1024,1024]{1,0:T(8,128)(2,1)} collective-permute-done((bf16[1024,1024]{1,0:T(8,128)(2,1)}, bf16[1024,1024]{1,0:T(8,128)(2,1)}, u32[]{:S(2)}, u32[]{:S(2)}) %collective-permute-start.4) | collective-permute-done | bytes 2097184 | tf_op jit(solution)/shard_map/ppermute | solution.py:10
  132.8 427.5 %while.22 = (s32[]{:T(128)}, f32[2,1024]{1,0:T(2,128)S(1)}, s32[1024]{0:T(1024)S(1)}, bf16[1024,1024]{1,0:T(8,128)(2,1)}, f32[2,1024]{1,0:T(2,128)S(1)}, /*index=5*/s32[]{:T(128)}, s32[]{:T(128)}) while((s32[]{:T(128)}, f32[2,1024]{1,0:T(2,128)S(1)}, s32[1024]{0:T(1024)S(1)}, bf16[1024,1024]{1,0:T(8,128)(2,1)}, ...), condition=%wide.region_1.2_spmd.clone, body=%wide.region_0.1_spmd.clone.sunk | while | flops 4204547 | bytes 2183295 | solution.py:66
  560.3 302.9 %while.23 = (s32[]{:T(128)}, f32[2,1024]{1,0:T(2,128)S(1)}, bf16[1024,1024]{1,0:T(8,128)(2,1)}, f32[2,1024]{1,0:T(2,128)S(1)}, s32[]{:T(128)}, /*index=5*/s32[]{:T(128)}) while((s32[]{:T(128)}, f32[2,1024]{1,0:T(2,128)S(1)}, bf16[1024,1024]{1,0:T(8,128)(2,1)}, f32[2,1024]{1,0:T(2,128)S(1)}, s32[]{:T(128)}, ...), condition=%wide.region_3.4_spmd.clone, body=%wide.region_2.3_spmd.clone.sunk | while | flops 4200451 | bytes 2146423 | solution.py:74
  584.7 6.3 collective-permute-start.1
  594.3 6.3 collective-permute-start.1
  603.9 6.3 collective-permute-start.1
  613.5 6.3 collective-permute-start.1
  623.1 6.3 collective-permute-start.1
  632.7 6.3 collective-permute-start.1
  642.3 6.3 collective-permute-start.1
  651.9 6.3 collective-permute-start.1
  661.5 6.3 collective-permute-start.1
  671.1 6.3 collective-permute-start.1
  680.7 6.3 collective-permute-start.1
  690.3 6.3 collective-permute-start.1
  699.9 6.3 collective-permute-start.1
  709.5 6.3 collective-permute-start.1
  719.1 6.3 collective-permute-start.1
  728.7 6.3 collective-permute-start.1
  738.3 6.3 collective-permute-start.1
  747.9 6.3 collective-permute-start.1
  757.5 6.3 collective-permute-start.1
  824.7 6.3 collective-permute-start.1
  (390 shorter events, 643.4 us)
Async XLA Ops:
  18.4 48.0 %collective-permute-start.3 = (bf16[1024,1024]{1,0:T(8,128)(2,1)}, bf16[1024,1024]{1,0:T(8,128)(2,1)}, u32[]{:S(2)}, u32[]{:S(2)}) collective-permute-start(bf16[1024,1024]{1,0:T(8,128)(2,1)} %subtract_convert_fusion.2), channel_id=1, source_target_pairs={{0,2},{1,3},{2,0},{3,1},{4,6},{5,7},{6,4},{7,5},{8,10},{9,11},{10,... | collective-permute-start | bytes 6291464 | tf_op jit(solution)/shard_map/ppermute | solution.py:10
  75.2 48.6 %collective-permute-start.4 = (bf16[1024,1024]{1,0:T(8,128)(2,1)}, bf16[1024,1024]{1,0:T(8,128)(2,1)}, u32[]{:S(2)}, u32[]{:S(2)}) collective-permute-start(bf16[1024,1024]{1,0:T(8,128)(2,1)} %subtract_convert_fusion.1), channel_id=1, source_target_pairs={{0,4},{1,5},{2,6},{3,7},{4,0},{5,1},{6,2},{7,3},{8,12},{9,13},{10,... | collective-permute-start | bytes 6291464 | tf_op jit(solution)/shard_map/ppermute | solution.py:10
  132.8 9.6 %collective-permute-start = (bf16[2,1024]{1,0:T(2,128)(2,1)S(1)}, bf16[2,1024]{1,0:T(2,128)(2,1)S(1)}, u32[]{:S(2)}, u32[]{:S(2)}) collective-permute-start(bf16[2,1024]{1,0:T(2,128)(2,1)S(1)} %broadcast_select_fusion.4), channel_id=1, source_target_pairs={{0,8},{8,16},{16,24},{24,32},{32,40},{40,48},{48,56},{56,64},{64,7... | collective-permute-start | bytes 12296 | tf_op jit(solution)/shard_map/while/body/eval_jaxpr/ppermute | solution.py:16
  584.7 7.6 collective-permute-start.1
  594.3 7.6 collective-permute-start.1
  603.9 7.6 collective-permute-start.1
  613.5 7.6 collective-permute-start.1
  623.1 7.6 collective-permute-start.1
  632.7 7.6 collective-permute-start.1
  642.3 7.6 collective-permute-start.1
  651.9 7.6 collective-permute-start.1
  671.1 7.6 collective-permute-start.1
  680.7 7.6 collective-permute-start.1
  699.9 7.6 collective-permute-start.1
  709.5 7.6 collective-permute-start.1
  728.7 7.6 collective-permute-start.1
  747.9 7.6 collective-permute-start.1
  757.5 7.6 collective-permute-start.1
  776.7 7.6 collective-permute-start.1
  786.3 7.6 collective-permute-start.1
  805.5 7.6 collective-permute-start.1
  824.7 7.6 collective-permute-start.1
  834.3 7.6 collective-permute-start.1
  853.5 7.6 collective-permute-start.1
  (47 other events, 343.9 us)
where the time goes:
time: 868 us; the launch traced here: 864 us
  waiting for transfers between devices  322 us (37%)
  starting transfers between devices  263 us (30%)
  matrix products  151 us (17%)
  local copies, waits for them, and re-layouts  110 us (13%)
  other arithmetic  15.1 us (2%)
    ppermute x64, starting transfers between devices, shifted(): return lax.ppermute(block, axis, route)  258 us
    ppermute x64, waiting for transfers between devices, shifted(): return lax.ppermute(block, axis, route)  225 us
    gather x32, local copies, waits for them, and re-layouts, down_step(): gathered = received[:, order_map].astype(jnp.bfloat16)  103 us
    ppermute x3, waiting for transfers between devices, partner_2(): return lax.ppermute(value, axis, pairs)  96.3 us
    dot_general x32, matrix products, down_step(): jnp.dot(gathered, merged.T, preferred_element_type=jnp.float32)  71.2 us
    dot_general x32, matrix products, up_step(): jnp.dot(received.astype(jnp.bfloat16), merged, preferred_element_type=jnp...  63.2 us
  transfers between devices with their start and end apart: 67, of which 67 were waited for; matrix products, arithmetic and copies ran while one was open for 0% of the time, Pallas kernels for 0%

commit v1 on v0

--- a/solution.py
+++ b/solution.py
@@ -1,19 +1,18 @@
 import jax
 import jax.numpy as jnp
 from jax import lax
+from jax.experimental import pallas as pl
+from jax.experimental.pallas import tpu as pltpu
 from jax.sharding import PartitionSpec as P
+
+MESH = pl.DeviceIdType.MESH
+NT = (((1,), (1,)), ((), ()))
 
 
 def partner_2(value, axis, distance):
     mask = 2**distance
     pairs = [(source, source ^ mask) for source in range(lax.axis_size(axis))]
     return lax.ppermute(value, axis, pairs)
-
-
-def shifted(block, axis, distance):
-    devices = range(lax.axis_size(axis))
-    route = [(i - distance, i) for i in devices if i - distance in devices]
-    return lax.ppermute(block, axis, route)
 
 
 def mask_map(one_map, one_pattern):
@@ -37,14 +36,82 @@
     )
 
 
+def sweep_kernel(layers, coupling, m_ref, idx_ref, src_ref, out_ref, a_ref, send_buf, down_buf, up_buf, sems):
+    me = lax.axis_index("layer")
+    box = lax.axis_index("box")
+    width = m_ref.shape[0]
+
+    barrier = pltpu.get_barrier_semaphore()
+
+    for near in (lax.rem(me + 1, layers), lax.rem(me + layers - 1, layers)):
+        pl.semaphore_signal(barrier, inc=1, device_id=(near, box), device_id_type=MESH)
+    pl.semaphore_wait(barrier, 2)
+
+    rows = 256
+
+    @pl.loop(0, width // rows)
+    def _(step):
+        base = pl.multiple_of(step * rows, rows)
+        spot = lax.broadcasted_iota(jnp.int32, (rows, width), 0) + base
+        onehot = (spot == idx_ref[...]).astype(jnp.float32).astype(jnp.bfloat16)
+        a_ref[pl.ds(base, rows), :] = lax.dot_general(
+            onehot, m_ref[...], NT, preferred_element_type=jnp.float32
+        ).astype(jnp.bfloat16)
+
+    def to(buf, slot, where):
+        return pltpu.make_async_remote_copy(
+            src_ref=send_buf.at[slot],
+            dst_ref=buf,
+            send_sem=sems.at[slot],
+            recv_sem=sems.at[2 + slot],
+            device_id=(where, box),
+            device_id_type=MESH,
+        )
+
+    down_copy = to(down_buf, 0, jnp.minimum(me + 1, layers - 1))
+    up_copy = to(up_buf, 1, jnp.maximum(me - 1, 0))
+
+    @pl.when(me == 0)
+    def _():
+        out_ref[...] = src_ref[...]
+
+    @pl.when(me > 0)
+    def _():
+        down_copy.wait_recv()
+        out_ref[...] = src_ref[...] + coupling * jnp.dot(
+            down_buf[...], a_ref[...], preferred_element_type=jnp.float32
+        )
+
+    @pl.when(me < layers - 1)
+    def _():
+        send_buf[0] = out_ref[...].astype(jnp.bfloat16)
+        down_copy.start()
+        up_copy.wait_recv()
+        out_ref[...] += coupling * jnp.dot(
+            up_buf[...], m_ref[...], preferred_element_type=jnp.float32
+        )
+
+    @pl.when(me > 0)
+    def _():
+        send_buf[1] = out_ref[...].astype(jnp.bfloat16)
+        up_copy.start()
+
+    @pl.when(me < layers - 1)
+    def _():
+        down_copy.wait_send()
+
+    @pl.when(me > 0)
+    def _():
+        up_copy.wait_send()
+
+
 def on_device(box_maps, block_pattern, face_inverses, index_map, sources):
     boxes = lax.axis_size("box")
     layers = lax.axis_size("layer")
     coupling = float(boxes) ** 0.5
     levels = boxes.bit_length() - 1
-    leaf = mask_map(box_maps[0], block_pattern[0])
     inverses = face_inverses[0]
-    current = leaf
+    current = mask_map(box_maps[0], block_pattern[0])
     position = lax.axis_index("box")
     for level in range(levels):
         partner = partner_2(current, "box", level)
@@ -52,26 +119,26 @@
         chosen = lax.dynamic_index_in_dim(inverses, tree_node, 0, keepdims=False)
         current = combine(current, partner, chosen, level)
     merged = current
-    source_rows = sources[0]
-    order_map = index_map[0]
-    initial = jnp.zeros(source_rows.shape, jnp.float32)
-
-    def down_step(step, state):
-        received = shifted(state, "layer", 1)
-        gathered = received[:, order_map].astype(jnp.bfloat16)
-        return source_rows + coupling * jnp.dot(
-            gathered, merged.T, preferred_element_type=jnp.float32
-        )
-
-    downward = lax.fori_loop(0, layers, down_step, initial)
-
-    def up_step(step, state):
-        received = shifted(state, "layer", -1)
-        return downward + coupling * jnp.dot(
-            received.astype(jnp.bfloat16), merged, preferred_element_type=jnp.float32
-        )
-
-    upward = lax.fori_loop(0, layers, up_step, initial)
+    width = merged.shape[0]
+    rhs = sources.shape[1]
+    import functools
+    vmem = pl.BlockSpec(memory_space=pltpu.VMEM)
+    upward = pl.pallas_call(
+        functools.partial(sweep_kernel, layers, coupling),
+        out_shape=jax.ShapeDtypeStruct((rhs, width), jnp.float32),
+        in_specs=[vmem] * 3,
+        out_specs=vmem,
+        scratch_shapes=[
+            pltpu.VMEM((width, width), jnp.bfloat16),
+            pltpu.VMEM((2, rhs, width), jnp.bfloat16),
+            pltpu.VMEM((rhs, width), jnp.bfloat16),
+            pltpu.VMEM((rhs, width), jnp.bfloat16),
+            pltpu.SemaphoreType.DMA((4,)),
+        ],
+        compiler_params=pltpu.CompilerParams(
+            collective_id=0, has_side_effects=True, vmem_limit_bytes=48 * 2**20
+        ),
+    )(merged, index_map, sources[0])
     return (merged[None], upward[None])
 
 

time: 868 us -> 341 us (0.39)
  the two profiles are of different devices: /device:TPU:6 before, /device:TPU:8 now
where the time goes in v1:
time: 341 us
  Pallas kernels  208 us (61%)
  waiting for transfers between devices  97.8 us (29%)
  matrix products  16.3 us (5%)
  other arithmetic  13.5 us (4%)
  starting transfers between devices  4.04 us (1%)
    pallas_call x1, Pallas kernels, on_device(): pl.pallas_call(functools.partial(sweep_kernel, layers, coupling), out_sha...  208 us
    ppermute x3, waiting for transfers between devices, partner_2(): return lax.ppermute(value, axis, pairs)  97.8 us
    dot_general x3, matrix products, combine(): jnp.dot(product, right_rows, precision=lax.Precision.HIGHEST)  13.3 us
    mul x3, other arithmetic, combine(): joined = 0.5 * (first.astype(jnp.float32) + second.astype(jnp.float32))  9.47 us
  transfers between devices with their start and end apart: 3, of which 3 were waited for; matrix products, arithmetic and copies ran while one was open for 0% of the time, Pallas kernels for 0%

profile of v1, /device:TPU:8, one launch (start us, length us, event | category | flops | bytes accessed | tf_op | source)
XLA Modules:
  0.0 341.0 jit_solution(8137518262499745883)
XLA Ops:
  0.6 0.0 copy-start
  0.6 0.8 convert_bitcast_fusion
  1.5 0.3 mul.20
  1.8 3.2 bitcast_multiply_fusion
  5.0 0.0 collective-permute-start
  5.0 4.5 %collective-permute-done = bf16[1024,1024]{1,0:T(8,128)(2,1)} collective-permute-done((bf16[1024,1024]{1,0:T(8,128)(2,1)}, bf16[1024,1024]{1,0:T(8,128)(2,1)}, u32[]{:S(2)}, u32[]{:S(2)}) %collective-permute-start) | collective-permute-done | bytes 2097184 | tf_op jit(solution)/shard_map/ppermute | solution.py:15
  9.5 3.2 add_multiply_fusion.2
  12.7 1.0 fusion.7
  13.7 4.7 %subtract_convert_fusion.2 = bf16[1024,1024]{1,0:T(8,128)(2,1)} fusion(f32[1024,1024]{1,0:T(8,128)S(1)} %add_multiply_fusion.2, f32[1024,256]{1,0:T(8,128)S(1)} %fusion.7), kind=kOutput, calls=%fused_computation.4 | convolution fusion | flops 3223322624 | bytes 8388608 | tf_op jit(solution)/shard_map/dot_general | solution.py:34
  18.4 2.2 collective-permute-start.1
  20.5 46.2 %collective-permute-done.1 = bf16[1024,1024]{1,0:T(8,128)(2,1)} collective-permute-done((bf16[1024,1024]{1,0:T(8,128)(2,1)}, bf16[1024,1024]{1,0:T(8,128)(2,1)}, u32[]{:S(2)}, u32[]{:S(2)}) %collective-permute-start.1) | collective-permute-done | bytes 2097184 | tf_op jit(solution)/shard_map/ppermute | solution.py:15
  66.8 3.2 add_multiply_fusion.1
  69.9 1.0 fusion.4
  71.0 4.7 %subtract_convert_fusion.1 = bf16[1024,1024]{1,0:T(8,128)(2,1)} fusion(f32[1024,1024]{1,0:T(8,128)S(1)} %add_multiply_fusion.1, f32[1024,256]{1,0:T(8,128)S(1)} %fusion.4), kind=kOutput, calls=%fused_computation.2 | convolution fusion | flops 3223322624 | bytes 8388608 | tf_op jit(solution)/shard_map/dot_general | solution.py:34
  75.7 1.9 collective-permute-start.2
  77.5 47.0 %collective-permute-done.2 = bf16[1024,1024]{1,0:T(8,128)(2,1)} collective-permute-done((bf16[1024,1024]{1,0:T(8,128)(2,1)}, bf16[1024,1024]{1,0:T(8,128)(2,1)}, u32[]{:S(2)}, u32[]{:S(2)}) %collective-permute-start.2) | collective-permute-done | bytes 2097184 | tf_op jit(solution)/shard_map/ppermute | solution.py:15
  124.6 3.2 add_multiply_fusion
  127.7 0.0 copy-start.2
  127.7 0.0 copy-start.3
  127.8 1.0 fusion.1
  128.8 3.9 %subtract_convert_fusion.m_ref = bf16[1024,1024]{1,0:T(8,128)(2,1)S(1)} fusion(f32[1024,1024]{1,0:T(8,128)S(1)} %add_multiply_fusion, f32[1024,256]{1,0:T(8,128)S(1)} %fusion.1), kind=kOutput, calls=%fused_computation | convolution fusion | flops 3223322624 | bytes 8388608 | tf_op jit(solution)/shard_map/dot_general | solution.py:34
  132.7 0.0 copy-start.1
  132.7 207.7 %shard_map.68 = f32[2,1024]{1,0:T(2,128)S(1)} custom-call(bf16[1024,1024]{1,0:T(8,128)(2,1)S(1)} %subtract_convert_fusion.m_ref, s32[1,1024]{1,0:T(1,128)S(1)} %copy-done.3, f32[2,1024]{1,0:T(2,128)S(1)} %bitcast.25), custom_call_target="tpu_custom_call" | custom-call | tf_op jit(solution)/shard_map/pallas_call | solution.py:126
  340.4 0.6 copy.10
  (4 shorter events, 0.0 us)
Async XLA Ops:
  0.6 12.0 %copy-start = (f32[1,7,256,256]{3,2,1,0:T(8,128)S(1)}, f32[1,7,256,256]{3,2,1,0:T(8,128)}, u32[]{:S(2)}) copy-start(f32[1,7,256,256]{3,2,1,0:T(8,128)} %param.7) | copy-start | bytes 5505028
  5.0 4.5 %collective-permute-start = (bf16[1024,1024]{1,0:T(8,128)(2,1)}, bf16[1024,1024]{1,0:T(8,128)(2,1)}, u32[]{:S(2)}, u32[]{:S(2)}) collective-permute-start(bf16[1024,1024]{1,0:T(8,128)(2,1)} %bitcast_multiply_fusion), channel_id=1, source_target_pairs={{0,1},{1,0},{2,3},{3,2},{4,5},{5,4},{6,7},{7,6},{8,9},{9,8},{10,11... | collective-permute-start | bytes 6291464 | tf_op jit(solution)/shard_map/ppermute | solution.py:15
  18.4 48.4 %collective-permute-start.1 = (bf16[1024,1024]{1,0:T(8,128)(2,1)}, bf16[1024,1024]{1,0:T(8,128)(2,1)}, u32[]{:S(2)}, u32[]{:S(2)}) collective-permute-start(bf16[1024,1024]{1,0:T(8,128)(2,1)} %subtract_convert_fusion.2), channel_id=1, source_target_pairs={{0,2},{1,3},{2,0},{3,1},{4,6},{5,7},{6,4},{7,5},{8,10},{9,11},{10,... | collective-permute-start | bytes 6291464 | tf_op jit(solution)/shard_map/ppermute | solution.py:15
  75.7 48.9 %collective-permute-start.2 = (bf16[1024,1024]{1,0:T(8,128)(2,1)}, bf16[1024,1024]{1,0:T(8,128)(2,1)}, u32[]{:S(2)}, u32[]{:S(2)}) collective-permute-start(bf16[1024,1024]{1,0:T(8,128)(2,1)} %subtract_convert_fusion.1), channel_id=1, source_target_pairs={{0,4},{1,5},{2,6},{3,7},{4,0},{5,1},{6,2},{7,3},{8,12},{9,13},{10,... | collective-permute-start | bytes 6291464 | tf_op jit(solution)/shard_map/ppermute | solution.py:15
  127.7 4.9 %copy-start.2 = (f32[1,2,1024]{2,1,0:T(2,128)S(1)}, f32[1,2,1024]{2,1,0:T(2,128)}, u32[]{:S(2)}) copy-start(f32[1,2,1024]{2,1,0:T(2,128)} %param.9) | copy-start | bytes 24580
  127.7 4.9 %copy-start.3 = (s32[1,1024]{1,0:T(1,128)S(1)}, s32[1,1024]{1,0:T(1,128)}, u32[]{:S(2)}) copy-start(s32[1,1024]{1,0:T(1,128)} %idx_ref.1) | copy-start | bytes 12292
  132.7 208.3 %copy-start.1 = (bf16[1024,1024]{1,0:T(8,128)(2,1)}, bf16[1024,1024]{1,0:T(8,128)(2,1)S(1)}, u32[]{:S(2)}) copy-start(bf16[1024,1024]{1,0:T(8,128)(2,1)S(1)} %subtract_convert_fusion.m_ref) | copy-start | bytes 6291460

commit v2 on v1

v2 whole, which is shorter than its diff:
```python
import functools
import math

import jax
import jax.numpy as jnp
from jax import lax
from jax.experimental import pallas as pl
from jax.experimental.pallas import tpu as pltpu
from jax.sharding import PartitionSpec as P

MESH = pl.DeviceIdType.MESH
NT = (((1,), (1,)), ((), ()))
F32 = jnp.float32
BF16 = jnp.bfloat16
CH = 128
ORDER = (2, 4, 0, 6)


def kernel(
    layers, coupling, map_ref, keep_ref, inv_ref, idx_ref, src_ref,
    m_ref, out_ref,
    leaf, part0, half1, part1, half2, part2, v_ref, pick, a_ref,
    send_buf, down_buf, up_buf,
    s0, r0, s1, r1, s2, r2, q1, q2, sems,
):
    me = lax.axis_index("layer")
    box = lax.axis_index("box")
    width = m_ref.shape[0]
    face = inv_ref.shape[1]
    core = lax.rem(box, 2)
    chip = box // 2
    sibling = box + 1 - 2 * core
    pair = 2 * (chip + 1 - 2 * lax.rem(chip, 2)) + core
    cross = 2 * (3 - chip) + core

    barrier = pltpu.get_barrier_semaphore()
    for near in (lax.rem(me + 1, layers), lax.rem(me + layers - 1, layers)):
        pl.semaphore_signal(barrier, inc=1, device_id=(near, box), device_id_type=MESH)
    for mate in (sibling, pair, cross):
        pl.semaphore_signal(barrier, inc=1, device_id=(me, mate), device_id_type=MESH)
    pl.semaphore_wait(barrier, 5)

    def rows(k):
        return pl.ds(pl.multiple_of(k * CH, CH), CH)

    def send(src, dst, k, ssem, rsem, mate):
        return pltpu.make_async_remote_copy(
            src_ref=src.at[rows(k), :], dst_ref=dst.at[rows(k), :],
            send_sem=ssem.at[k], recv_sem=rsem.at[k],
            device_id=(me, mate), device_id_type=MESH,
        )

    def joined(own, other, where):
        return 0.5 * (own[where, :].astype(F32) + other[where, :].astype(F32))

    def make_v(level, own, other):
        for part in range(face // CH):
            where = pl.ds(level * face + part * CH, CH)
            v_ref[level, pl.ds(part * CH, CH), :] = joined(own, other, where).astype(BF16)

    places = (3 + box // 2, 1 + box // 4, 0)

    def merge(level, own, other, out, k):
        whole = joined(own, other, rows(k))
        left = whole[:, level * face : (level + 1) * face].astype(BF16)
        inner = inv_ref[places[level]].astype(BF16)
        product = jnp.dot(left, inner, preferred_element_type=F32).astype(BF16)
        out[rows(k), :] = (
            whole - jnp.dot(product, v_ref[level], preferred_element_type=F32)
        ).astype(BF16)

    for k in range(width // CH):
        leaf[rows(k), :] = (map_ref[rows(k), :].astype(F32) * keep_ref[pl.ds(k, 1), :]).astype(BF16)
        send(leaf, part0, k, s0, r0, sibling).start()

    @pl.loop(0, width // CH)
    def _(step):
        spot = lax.broadcasted_iota(jnp.int32, (CH, width), 0) + step * CH
        pick[rows(step), :] = (spot == idx_ref[...]).astype(F32).astype(BF16)

    def got(buf, k, ssem, rsem, mate):
        send(buf, buf, k, ssem, rsem, mate).wait_recv()

    for k in range(2):
        got(part0, k, s0, r0, sibling)
    make_v(0, leaf, part0)
    for k in range(2, width // CH):
        got(part0, k, s0, r0, sibling)
    for base in ORDER:
        mine, theirs = base + core, base + 1 - core
        merge(0, leaf, part0, half1, mine)
        send(half1, part1, mine, s1, r1, pair).start()
        merge(0, leaf, part0, half1, theirs)

    def permute(k):
        a_ref[:, rows(k)] = lax.dot_general(
            pick[...], m_ref[rows(k), :], NT, preferred_element_type=F32
        ).astype(BF16)

    def last(step):
        mine, theirs = ORDER[step] + core, ORDER[step] + 1 - core
        got(part2, mine, s2, r2, cross)
        send(part2, part2, mine, q2, r2, sibling).start()
        got(part2, theirs, q2, r2, sibling)
        if step == 0:
            return
        if step == 1:
            make_v(2, half2, part2)
        for other in (0, 1) if step == 1 else (step,):
            for k in (ORDER[other], ORDER[other] + 1):
                merge(2, half2, part2, m_ref, k)
                permute(k)

    for step, base in enumerate(ORDER):
        mine, theirs = base + core, base + 1 - core
        got(part1, mine, s1, r1, pair)
        send(part1, part1, mine, q1, r1, sibling).start()
        if step == 0:
            got(part1, theirs, q1, r1, sibling)
            make_v(1, half1, part1)
        merge(1, half1, part1, half2, mine)
        send(half2, part2, mine, s2, r2, cross).start()
        if step > 0:
            got(part1, theirs, q1, r1, sibling)
        merge(1, half1, part1, half2, theirs)
        if step > 0:
            last(step - 1)
    last(len(ORDER) - 1)

    def to(buf, slot, where):
        return pltpu.make_async_remote_copy(
            src_ref=send_buf.at[slot],
            dst_ref=buf,
            send_sem=sems.at[slot],
            recv_sem=sems.at[2 + slot],
            device_id=(where, box),
            device_id_type=MESH,
        )

    down_copy = to(down_buf, 0, jnp.minimum(me + 1, layers - 1))
    up_copy = to(up_buf, 1, jnp.maximum(me - 1, 0))

    @pl.when(me == 0)
    def _():
        out_ref[...] = src_ref[...]

    @pl.when(me > 0)
    def _():
        down_copy.wait_recv()
        out_ref[...] = src_ref[...] + coupling * jnp.dot(
            down_buf[...], a_ref[...], preferred_element_type=jnp.float32
        )

    @pl.when(me < layers - 1)
    def _():
        send_buf[0] = out_ref[...].astype(jnp.bfloat16)
        down_copy.start()
        up_copy.wait_recv()
        out_ref[...] += coupling * jnp.dot(
            up_buf[...], m_ref[...], preferred_element_type=jnp.float32
        )

    @pl.when(me > 0)
    def _():
        send_buf[1] = out_ref[...].astype(jnp.bfloat16)
        up_copy.start()

    @pl.when(me < layers - 1)
    def _():
        down_copy.wait_send()

    @pl.when(me > 0)
    def _():
        up_copy.wait_send()

    for k in range(width // CH):
        send(leaf, part0, k, s0, r0, sibling).wait_send()
    for base in ORDER:
        mine = base + core
        send(half1, part1, mine, s1, r1, pair).wait_send()
        send(half2, part2, mine, s2, r2, cross).wait_send()
        send(part1, part1, mine, q1, r1, sibling).wait_send()
        send(part2, part2, mine, q2, r2, sibling).wait_send()


def on_device(box_maps, block_pattern, face_inverses, index_map, sources):
    boxes = lax.axis_size("box")
    layers = lax.axis_size("layer")
    coupling = math.sqrt(boxes)
    width = box_maps.shape[2]
    rhs = sources.shape[1]
    face = face_inverses.shape[2]
    keep = jnp.repeat(block_pattern[0].astype(F32), width // block_pattern.shape[2], axis=1)
    vmem = pl.BlockSpec(memory_space=pltpu.VMEM)
    square = pltpu.VMEM((width, width), BF16)
    count = pltpu.SemaphoreType.DMA((width // CH,))
    merged, upward = pl.pallas_call(
        functools.partial(kernel, layers, coupling),
        out_shape=(
            jax.ShapeDtypeStruct((width, width), BF16),
            jax.ShapeDtypeStruct((rhs, width), F32),
        ),
        in_specs=[vmem] * 5,
        out_specs=(vmem, vmem),
        scratch_shapes=[square] * 6
        + [pltpu.VMEM((3, face, width), BF16), square, square]
        + [
            pltpu.VMEM((2, rhs, width), BF16),
            pltpu.VMEM((rhs, width), BF16),
            pltpu.VMEM((rhs, width), BF16),
        ]
        + [count] * 8
        + [pltpu.SemaphoreType.DMA((4,))],
        compiler_params=pltpu.CompilerParams(
            collective_id=0, has_side_effects=True, vmem_limit_bytes=56 * 2**20
        ),
    )(box_maps[0], keep, face_inverses[0], index_map, sources[0])
    return (merged[None], upward[None])


def solution(mesh):
    return jax.shard_map(
        on_device,
        mesh=mesh,
        in_specs=(
            P("layer", "box", None),
            P("layer", "box", None),
            P("layer", None, None, None),
            P("layer", None),
            P("layer", "box", None),
        ),
        out_specs=(P("layer", None, None), P("layer", "box", None)),
        check_vma=False,
    )
```

time: 341 us -> 258 us (0.76)
  the two profiles are of different devices: /device:TPU:8 before, /device:TPU:24 now
where the time goes in v2:
time: 258 us
  Pallas kernels  252 us (98%)
  local copies, waits for them, and re-layouts  4.45 us (2%)
    pallas_call x1, Pallas kernels, on_device(): pl.pallas_call(functools.partial(kernel, layers, coupling), out_shape=(ja...  252 us

profile of v2, /device:TPU:24, one launch (start us, length us, event | category | flops | bytes accessed | tf_op | source)
XLA Modules:
  0.0 257.5 jit_solution(1491432619806581811)
XLA Ops:
  0.6 0.7 convert_bitcast_fusion
  1.3 0.1 copy.7
  1.4 0.7 broadcast_bitcast_fusion.keep_ref
  2.1 251.7 %shard_map.68 = (bf16[1024,1024]{1,0:T(8,128)(2,1)}, f32[2,1024]{1,0:T(2,128)}) custom-call(bf16[1024,1024]{1,0:T(8,128)(2,1)} %bitcast.9, f32[8,1024]{1,0:T(8,128)} %broadcast_bitcast_fusion.keep_ref, f32[7,256,256]{2,1,0:T(8,128)} %bitcast.11, s32[1,1024]{1,0:T(1,128)} %idx_ref.1, f32[2,1024]{1,0:T(2,128)} %bitcast.12), custom_call_target="tpu_custom_call" | custom-call | tf_op jit(solution)/shard_map/pallas_call | solution.py:197
  253.8 0.0 copy-start
  253.8 3.1 %copy.10 = bf16[1,1024,1024]{2,1,0:T(8,128)(2,1)} copy(bf16[1,1024,1024]{2,1,0:T(8,128)(2,1)} %bitcast.10) | data formatting | bytes 4194304
  256.9 0.0 copy-done
  256.9 0.6 copy.11
Async XLA Ops:
  253.8 3.1 %copy-start = (f32[2,1024]{1,0:T(2,128)S(1)}, f32[2,1024]{1,0:T(2,128)}, u32[]{:S(2)}) copy-start(f32[2,1024]{1,0:T(2,128)} %get-tuple-element.5) | copy-start | bytes 24580

commit v3 on v2

--- a/solution.py
+++ b/solution.py
@@ -20,8 +20,12 @@
     layers, coupling, map_ref, keep_ref, inv_ref, idx_ref, src_ref,
     m_ref, out_ref,
     leaf, part0, half1, part1, half2, part2, v_ref, pick, a_ref,
-    send_buf, down_buf, up_buf,
-    s0, r0, s1, r1, s2, r2, q1, q2, sems,
+    d_ref, u_ref, send_d, send_u, down_buf, up_buf,
+    phi, phi_in, psi, psi_in, res, res_in,
+    dcol, ucol, flat, part3, link_d, link_u, in_d, in_u, col16, last_in,
+    s0, r0, s1, r1, s2, r2, q1, q2,
+    phi_s, phi_r, psi_s, psi_r, res_s, res_r, one_s, one_r,
+    ld_s, ld_r, lu_s, lu_r, bd_s, bu_s, f_s, f_r,
 ):
     me = lax.axis_index("layer")
     box = lax.axis_index("box")
@@ -33,12 +37,31 @@
     pair = 2 * (chip + 1 - 2 * lax.rem(chip, 2)) + core
     cross = 2 * (3 - chip) + core
 
+    depth = 8
+    blocks = layers // depth
+    boxes = 8
+    group = me // depth
+    z = lax.rem(me, depth)
+    first, final = z == 0, z == depth - 1
+    top, bottom = group == 0, group == blocks - 1
+
     barrier = pltpu.get_barrier_semaphore()
-    for near in (lax.rem(me + 1, layers), lax.rem(me + layers - 1, layers)):
-        pl.semaphore_signal(barrier, inc=1, device_id=(near, box), device_id_type=MESH)
-    for mate in (sibling, pair, cross):
-        pl.semaphore_signal(barrier, inc=1, device_id=(me, mate), device_id_type=MESH)
-    pl.semaphore_wait(barrier, 5)
+
+    def greet(layer, mate):
+        pl.semaphore_signal(barrier, inc=1, device_id=(layer, mate), device_id_type=MESH)
+
+    for step in range(1, boxes):
+        greet(me, lax.rem(box + step, boxes))
+    for step in range(1, depth):
+        greet(group * depth + lax.rem(z + step, depth), box)
+    for step in (1, blocks - 1):
+        for mate in range(boxes):
+            greet(lax.rem(group + step, blocks) * depth + z, mate)
+    for k in range(width // CH):
+        leaf[pl.ds(k * CH, CH), :] = (
+            map_ref[pl.ds(k * CH, CH), :].astype(F32) * keep_ref[pl.ds(k, 1), :]
+        ).astype(BF16)
+    pl.semaphore_wait(barrier, boxes - 1 + depth - 1 + 2 * boxes)
 
     def rows(k):
         return pl.ds(pl.multiple_of(k * CH, CH), CH)
@@ -70,7 +93,6 @@
         ).astype(BF16)
 
     for k in range(width // CH):
-        leaf[rows(k), :] = (map_ref[rows(k), :].astype(F32) * keep_ref[pl.ds(k, 1), :]).astype(BF16)
         send(leaf, part0, k, s0, r0, sibling).start()
 
     @pl.loop(0, width // CH)
@@ -127,51 +149,257 @@
             last(step - 1)
     last(len(ORDER) - 1)
 
-    def to(buf, slot, where):
+    def dot(x, y):
+        return jnp.dot(x, y, preferred_element_type=F32)
+
+    def finite(y):
+        return jnp.where(jnp.abs(y) < 1e37, y, 0.0).astype(BF16)
+
+    below, above = jnp.minimum(me + 1, layers - 1), jnp.maximum(me - 1, 0)
+    nblk = phi_s.shape[0]
+    rb = CH // nblk
+
+    def hop(src, dst, ssem, rsem, where, mate):
         return pltpu.make_async_remote_copy(
-            src_ref=send_buf.at[slot],
-            dst_ref=buf,
-            send_sem=sems.at[slot],
-            recv_sem=sems.at[2 + slot],
-            device_id=(where, box),
-            device_id_type=MESH,
+            src_ref=src, dst_ref=dst, send_sem=ssem, recv_sem=rsem,
+            device_id=(where, mate), device_id_type=MESH,
         )
 
-    down_copy = to(down_buf, 0, jnp.minimum(me + 1, layers - 1))
-    up_copy = to(up_buf, 1, jnp.maximum(me - 1, 0))
-
-    @pl.when(me == 0)
-    def _():
-        out_ref[...] = src_ref[...]
-
-    @pl.when(me > 0)
-    def _():
-        down_copy.wait_recv()
-        out_ref[...] = src_ref[...] + coupling * jnp.dot(
-            down_buf[...], a_ref[...], preferred_element_type=jnp.float32
-        )
-
-    @pl.when(me < layers - 1)
-    def _():
-        send_buf[0] = out_ref[...].astype(jnp.bfloat16)
-        down_copy.start()
-        up_copy.wait_recv()
-        out_ref[...] += coupling * jnp.dot(
-            up_buf[...], m_ref[...], preferred_element_type=jnp.float32
-        )
-
-    @pl.when(me > 0)
-    def _():
-        send_buf[1] = out_ref[...].astype(jnp.bfloat16)
-        up_copy.start()
-
-    @pl.when(me < layers - 1)
-    def _():
-        down_copy.wait_send()
-
-    @pl.when(me > 0)
-    def _():
-        up_copy.wait_send()
+    def strip(j):
+        return pl.ds(j * rb, rb)
+
+    def phi_copy(j):
+        return hop(phi.at[strip(j), :], phi_in.at[strip(j), :], phi_s.at[j], phi_r.at[j], below, box)
+
+    def psi_copy(j):
+        return hop(psi.at[strip(j), :], psi_in.at[strip(j), :], psi_s.at[j], psi_r.at[j], above, box)
+
+    def res_copy(j):
+        return hop(res.at[strip(j), :], res_in.at[strip(j), :], res_s.at[j], res_r.at[j], above, box)
+
+    d_copy = hop(send_d, down_buf, one_s.at[0], one_r.at[0], below, box)
+    u_copy = hop(send_u, up_buf, one_s.at[1], one_r.at[1], above, box)
+
+    def own_rows(j):
+        return pl.ds(pl.multiple_of(box * CH + j * rb, rb), rb)
+
+    def phi_stream():
+        @pl.when(first)
+        def _():
+            d_ref[...] = src_ref[...]
+
+        @pl.when(jnp.logical_not(first))
+        def _():
+            d_copy.wait_recv()
+            d_ref[...] = src_ref[...] + coupling * dot(down_buf[...], a_ref[...])
+
+        @pl.when(jnp.logical_not(final))
+        def _():
+            send_d[...] = d_ref[...].astype(BF16)
+            d_copy.start()
+
+        @pl.when(final)
+        def _():
+            send_u[...] = d_ref[...].astype(BF16)
+            u_copy.start()
+
+        for j in range(nblk):
+            @pl.when(first)
+            def _():
+                phi[strip(j), :] = (coupling * a_ref[own_rows(j), :].astype(F32)).astype(BF16)
+
+            @pl.when(jnp.logical_not(first))
+            def _():
+                phi_copy(j).wait_recv()
+                phi[strip(j), :] = finite(coupling * dot(phi_in[strip(j), :], a_ref[...]))
+
+            @pl.when(jnp.logical_not(final))
+            def _():
+                phi_copy(j).start()
+
+            @pl.when(final)
+            def _():
+                res[strip(j), :] = phi[strip(j), :]
+                res_copy(j).start()
+
+    def psi_stream():
+        for j in range(nblk):
+            @pl.when(final)
+            def _():
+                psi[strip(j), :] = (coupling * m_ref[own_rows(j), :].astype(F32)).astype(BF16)
+
+            @pl.when(jnp.logical_not(final))
+            def _():
+                psi_copy(j).wait_recv()
+                psi[strip(j), :] = finite(coupling * dot(psi_in[strip(j), :], m_ref[...]))
+
+            @pl.when(jnp.logical_not(first))
+            def _():
+                psi_copy(j).start()
+
+    @pl.when(z < depth // 2)
+    def _():
+        phi_stream()
+        psi_stream()
+
+    @pl.when(z >= depth // 2)
+    def _():
+        psi_stream()
+        phi_stream()
+
+    def spread(copy_of, begin):
+        for step in range(1, depth):
+            copy = copy_of(step)
+            copy.start() if begin else copy.wait_send()
+
+    def d_spread(step):
+        return hop(dcol, dcol, bd_s.at[step], bd_s.at[0],
+                   group * depth + lax.rem(z + step, depth), box)
+
+    def u_spread(step):
+        return hop(ucol, ucol, bu_s.at[step], bu_s.at[0],
+                   group * depth + lax.rem(z + step, depth), box)
+
+    def link_copy(link, buf, ssem, rsem, where, j):
+        return hop(link.at[:, :, pl.ds(j * CH, CH)], buf.at[box], ssem.at[j], rsem.at[box], where, j)
+
+    def gather_cols(link, buf, ssem, rsem, col):
+        for j in range(boxes):
+            hop(buf.at[j], buf.at[j], ssem.at[j], rsem.at[j], me, box).wait_recv()
+        total = buf[0]
+        for j in range(1, boxes):
+            total = total + buf[j]
+        for j in range(boxes):
+            col16[pl.ds(2 * j, 2), :] = total[j]
+        col[...] = col16[...].astype(BF16)
+
+    def unfold(value, link, mine):
+        flat[...] = value
+        for j in range(boxes):
+            part3[j] = flat[pl.ds(2 * j, 2), :]
+        if link is not None:
+            link[...] = part3[...]
+            link[box] += mine
+
+    after = jnp.minimum(group + 1, blocks - 1) * depth + z
+    before = jnp.maximum(group - 1, 0) * depth + z
+
+    @pl.when(top)
+    def _():
+        dcol[...] = jnp.zeros_like(dcol)
+
+    @pl.when(bottom)
+    def _():
+        ucol[...] = jnp.zeros_like(ucol)
+
+    @pl.when(final)
+    def _():
+        @pl.when(jnp.logical_not(top))
+        def _():
+            gather_cols(link_d, in_d, ld_s, ld_r, dcol)
+            spread(d_spread, True)
+
+        @pl.when(jnp.logical_not(bottom))
+        def _():
+            unfold(dot(dcol[...], phi[...]), link_d, d_ref[...])
+            for j in range(boxes):
+                link_copy(link_d, in_d, ld_s, ld_r, after, j).start()
+
+    @pl.when(final)
+    def _():
+        u_ref[...] = d_ref[...]
+
+    @pl.when(jnp.logical_not(final))
+    def _():
+        u_copy.wait_recv()
+        u_ref[...] = d_ref[...] + coupling * dot(up_buf[...], m_ref[...])
+
+        @pl.when(jnp.logical_not(first))
+        def _():
+            send_u[...] = u_ref[...].astype(BF16)
+            u_copy.start()
+
+        for j in range(nblk):
+            res_copy(j).wait_recv()
+            res[strip(j), :] = finite(
+                phi[strip(j), :].astype(F32) + coupling * dot(res_in[strip(j), :], m_ref[...])
+            )
+
+            @pl.when(jnp.logical_not(first))
+            def _():
+                res_copy(j).start()
+
+        @pl.when(jnp.logical_not(top))
+        def _():
+            d_spread(1).wait_recv()
+
+    @pl.when(first)
+    def _():
+        @pl.when(jnp.logical_not(bottom))
+        def _():
+            gather_cols(link_u, in_u, lu_s, lu_r, ucol)
+            spread(u_spread, True)
+
+        unfold(dot(dcol[...], res[...]) + dot(ucol[...], psi[...]), link_u, u_ref[...])
+
+        @pl.when(jnp.logical_not(top))
+        def _():
+            for j in range(boxes):
+                link_copy(link_u, in_u, lu_s, lu_r, before, j).start()
+
+    @pl.when(jnp.logical_not(first))
+    def _():
+        @pl.when(jnp.logical_not(bottom))
+        def _():
+            u_spread(1).wait_recv()
+
+        unfold(dot(dcol[...], res[...]) + dot(ucol[...], psi[...]), None, None)
+
+    def last_copy(step):
+        mate = lax.rem(box + step, boxes)
+        return hop(part3.at[mate], last_in.at[step], f_s.at[step], f_r.at[step], me, mate)
+
+    for step in range(1, boxes):
+        last_copy(step).start()
+    total = u_ref[...] + part3[box]
+    for step in range(1, boxes):
+        last_copy(step).wait_recv()
+        total = total + last_in[step]
+    out_ref[...] = total
+
+    for step in range(1, boxes):
+        last_copy(step).wait_send()
+
+    @pl.when(jnp.logical_not(final))
+    def _():
+        d_copy.wait_send()
+        for j in range(nblk):
+            phi_copy(j).wait_send()
+
+    @pl.when(jnp.logical_not(first))
+    def _():
+        u_copy.wait_send()
+        for j in range(nblk):
+            psi_copy(j).wait_send()
+            res_copy(j).wait_send()
+
+    @pl.when(jnp.logical_and(final, jnp.logical_not(top)))
+    def _():
+        spread(d_spread, False)
+
+    @pl.when(jnp.logical_and(final, jnp.logical_not(bottom)))
+    def _():
+        for j in range(boxes):
+            link_copy(link_d, in_d, ld_s, ld_r, after, j).wait_send()
+
+    @pl.when(jnp.logical_and(first, jnp.logical_not(bottom)))
+    def _():
+        spread(u_spread, False)
+
+    @pl.when(jnp.logical_and(first, jnp.logical_not(top)))
+    def _():
+        for j in range(boxes):
+            link_copy(link_u, in_u, lu_s, lu_r, before, j).wait_send()
 
     for k in range(width // CH):
         send(leaf, part0, k, s0, r0, sibling).wait_send()
@@ -204,13 +432,18 @@
         out_specs=(vmem, vmem),
         scratch_shapes=[square] * 6
         + [pltpu.VMEM((3, face, width), BF16), square, square]
-        + [
-            pltpu.VMEM((2, rhs, width), BF16),
-            pltpu.VMEM((rhs, width), BF16),
-            pltpu.VMEM((rhs, width), BF16),
-        ]
+        + [pltpu.VMEM((rhs, width), F32)] * 2
+        + [pltpu.VMEM((rhs, width), BF16)] * 4
+        + [pltpu.VMEM((CH, width), BF16)] * 6
+        + [pltpu.VMEM((boxes * rhs, CH), BF16)] * 2
+        + [pltpu.VMEM((boxes * rhs, width), F32)]
+        + [pltpu.VMEM((boxes, rhs, width), F32)] * 3
+        + [pltpu.VMEM((boxes, boxes, rhs, CH), F32)] * 2
+        + [pltpu.VMEM((boxes * rhs, CH), F32), pltpu.VMEM((boxes, rhs, width), F32)]
         + [count] * 8
-        + [pltpu.SemaphoreType.DMA((4,))],
+        + [pltpu.SemaphoreType.DMA((4,))] * 6
+        + [pltpu.SemaphoreType.DMA((2,))] * 2
+        + [pltpu.SemaphoreType.DMA((boxes,))] * 8,
         compiler_params=pltpu.CompilerParams(
             collective_id=0, has_side_effects=True, vmem_limit_bytes=56 * 2**20
         ),

time: 258 us -> 140 us (0.54)
  the two profiles are of different devices: /device:TPU:24 before, /device:TPU:33 now
where the time goes in v3:
time: 140 us
  Pallas kernels  134 us (96%)
  local copies, waits for them, and re-layouts  4.45 us (3%)
    pallas_call x1, Pallas kernels, on_device(): pl.pallas_call(functools.partial(kernel, layers, coupling), out_shape=(ja...  134 us
    unnamed x4, local copies, waits for them, and re-layouts  3.69 us

profile of v3, /device:TPU:33, one launch (start us, length us, event | category | flops | bytes accessed | tf_op | source)
XLA Modules:
  0.0 140.1 jit_solution(7682457453457026695)
XLA Ops:
  0.6 0.7 convert_bitcast_fusion
  1.3 0.1 copy.7
  1.4 0.7 broadcast_bitcast_fusion.keep_ref
  2.1 134.3 %shard_map.68 = (bf16[1024,1024]{1,0:T(8,128)(2,1)}, f32[2,1024]{1,0:T(2,128)}) custom-call(bf16[1024,1024]{1,0:T(8,128)(2,1)} %bitcast.9, f32[8,1024]{1,0:T(8,128)} %broadcast_bitcast_fusion.keep_ref, f32[7,256,256]{2,1,0:T(8,128)} %bitcast.11, s32[1,1024]{1,0:T(1,128)} %idx_ref.1, f32[2,1024]{1,0:T(2,128)} %bitcast.12), custom_call_target="tpu_custom_call" | custom-call | tf_op jit(solution)/shard_map/pallas_call | solution.py:425
  136.4 0.0 copy-start
  136.4 3.1 %copy.10 = bf16[1,1024,1024]{2,1,0:T(8,128)(2,1)} copy(bf16[1,1024,1024]{2,1,0:T(8,128)(2,1)} %bitcast.10) | data formatting | bytes 4194304
  139.5 0.0 copy-done
  139.5 0.6 copy.11
Async XLA Ops:
  136.4 3.1 %copy-start = (f32[2,1024]{1,0:T(2,128)S(1)}, f32[2,1024]{1,0:T(2,128)}, u32[]{:S(2)}) copy-start(f32[2,1024]{1,0:T(2,128)} %get-tuple-element.5) | copy-start | bytes 24580

commit v4 on v3

--- a/solution.py
+++ b/solution.py
@@ -17,8 +17,9 @@
 
 
 def kernel(
-    layers, coupling, map_ref, keep_ref, inv_ref, idx_ref, src_ref,
-    m_ref, out_ref,
+    layers, coupling, map_hbm, keep_ref, inv_hbm, idx_ref, src_ref,
+    m_hbm, out_ref,
+    m_ref, part0_in, inv_ref, io_sem,
     leaf, part0, half1, part1, half2, part2, v_ref, pick, a_ref,
     d_ref, u_ref, send_d, send_u, down_buf, up_buf,
     phi, phi_in, psi, psi_in, res, res_in,
@@ -31,6 +32,7 @@
     box = lax.axis_index("box")
     width = m_ref.shape[0]
     face = inv_ref.shape[1]
+    places = (3 + box // 2, 1 + box // 4, 0)
     core = lax.rem(box, 2)
     chip = box // 2
     sibling = box + 1 - 2 * core
@@ -57,10 +59,26 @@
     for step in (1, blocks - 1):
         for mate in range(boxes):
             greet(lax.rem(group + step, blocks) * depth + z, mate)
+    def load_map(k):
+        return pltpu.make_async_copy(
+            map_hbm.at[pl.ds(k * CH, CH), :], part0_in.at[pl.ds(k * CH, CH), :], io_sem.at[k]
+        )
+
+    def load_inverse(level):
+        return pltpu.make_async_copy(
+            inv_hbm.at[places[level]], inv_ref.at[level], io_sem.at[width // CH + level]
+        )
+
     for k in range(width // CH):
-        leaf[pl.ds(k * CH, CH), :] = (
-            map_ref[pl.ds(k * CH, CH), :].astype(F32) * keep_ref[pl.ds(k, 1), :]
-        ).astype(BF16)
+        load_map(k).start()
+    for level in range(3):
+        load_inverse(level).start()
+    for k in range(width // CH):
+        load_map(k).wait()
+        for j in range(width // CH):
+            kept = keep_ref[k, j].astype(F32)
+            block = (pl.ds(k * CH, CH), pl.ds(j * CH, CH))
+            leaf[block] = (part0_in[block].astype(F32) * kept).astype(BF16)
     pl.semaphore_wait(barrier, boxes - 1 + depth - 1 + 2 * boxes)
 
     def rows(k):
@@ -81,12 +99,10 @@
             where = pl.ds(level * face + part * CH, CH)
             v_ref[level, pl.ds(part * CH, CH), :] = joined(own, other, where).astype(BF16)
 
-    places = (3 + box // 2, 1 + box // 4, 0)
-
     def merge(level, own, other, out, k):
         whole = joined(own, other, rows(k))
         left = whole[:, level * face : (level + 1) * face].astype(BF16)
-        inner = inv_ref[places[level]].astype(BF16)
+        inner = inv_ref[level].astype(BF16)
         product = jnp.dot(left, inner, preferred_element_type=F32).astype(BF16)
         out[rows(k), :] = (
             whole - jnp.dot(product, v_ref[level], preferred_element_type=F32)
@@ -106,12 +122,16 @@
     for k in range(2):
         got(part0, k, s0, r0, sibling)
     make_v(0, leaf, part0)
-    for k in range(2, width // CH):
-        got(part0, k, s0, r0, sibling)
+    for level in range(3):
+        load_inverse(level).wait()
     for base in ORDER:
         mine, theirs = base + core, base + 1 - core
+        if base:
+            got(part0, mine, s0, r0, sibling)
         merge(0, leaf, part0, half1, mine)
         send(half1, part1, mine, s1, r1, pair).start()
+        if base:
+            got(part0, theirs, s0, r0, sibling)
         merge(0, leaf, part0, half1, theirs)
 
     def permute(k):
@@ -149,6 +169,9 @@
             last(step - 1)
     last(len(ORDER) - 1)
 
+    store_map = pltpu.make_async_copy(m_ref, m_hbm, io_sem.at[width // CH + 3])
+    store_map.start()
+
     def dot(x, y):
         return jnp.dot(x, y, preferred_element_type=F32)
 
@@ -166,7 +189,7 @@
         )
 
     def strip(j):
-        return pl.ds(j * rb, rb)
+        return pl.ds(pl.multiple_of(j * rb, rb), rb)
 
     def phi_copy(j):
         return hop(phi.at[strip(j), :], phi_in.at[strip(j), :], phi_s.at[j], phi_r.at[j], below, box)
@@ -203,7 +226,8 @@
             send_u[...] = d_ref[...].astype(BF16)
             u_copy.start()
 
-        for j in range(nblk):
+        @pl.loop(0, nblk)
+        def _(j):
             @pl.when(first)
             def _():
                 phi[strip(j), :] = (coupling * a_ref[own_rows(j), :].astype(F32)).astype(BF16)
@@ -223,7 +247,8 @@
                 res_copy(j).start()
 
     def psi_stream():
-        for j in range(nblk):
+        @pl.loop(0, nblk)
+        def _(j):
             @pl.when(final)
             def _():
                 psi[strip(j), :] = (coupling * m_ref[own_rows(j), :].astype(F32)).astype(BF16)
@@ -319,7 +344,8 @@
             send_u[...] = u_ref[...].astype(BF16)
             u_copy.start()
 
-        for j in range(nblk):
+        @pl.loop(0, nblk)
+        def _(j):
             res_copy(j).wait_recv()
             res[strip(j), :] = finite(
                 phi[strip(j), :].astype(F32) + coupling * dot(res_in[strip(j), :], m_ref[...])
@@ -367,19 +393,22 @@
         total = total + last_in[step]
     out_ref[...] = total
 
+    store_map.wait()
     for step in range(1, boxes):
         last_copy(step).wait_send()
 
     @pl.when(jnp.logical_not(final))
     def _():
         d_copy.wait_send()
-        for j in range(nblk):
+        @pl.loop(0, nblk)
+        def _(j):
             phi_copy(j).wait_send()
 
     @pl.when(jnp.logical_not(first))
     def _():
         u_copy.wait_send()
-        for j in range(nblk):
+        @pl.loop(0, nblk)
+        def _(j):
             psi_copy(j).wait_send()
             res_copy(j).wait_send()
 
@@ -411,6 +440,23 @@
         send(part2, part2, mine, q2, r2, sibling).wait_send()
 
 
+def hand_on(m_in, u_in, m_out, u_out, m_buf, u_buf, sem):
+    count = m_in.shape[0] // CH
+    pairs = [(m_in, m_buf, m_out, pl.ds(k * CH, CH)) for k in range(count)]
+    pairs.append((u_in, u_buf, u_out, pl.ds(0, u_in.shape[0])))
+    loads, stores = [], []
+    for k, (src, buf, dst, where) in enumerate(pairs):
+        loads.append(pltpu.make_async_copy(src.at[where, :], buf.at[where, :], sem.at[2 * k]))
+        stores.append(pltpu.make_async_copy(buf.at[where, :], dst.at[where, :], sem.at[2 * k + 1]))
+    for load in loads:
+        load.start()
+    for load, store in zip(loads, stores):
+        load.wait()
+        store.start()
+    for store in stores:
+        store.wait()
+
+
 def on_device(box_maps, block_pattern, face_inverses, index_map, sources):
     boxes = lax.axis_size("box")
     layers = lax.axis_size("layer")
@@ -418,8 +464,8 @@
     width = box_maps.shape[2]
     rhs = sources.shape[1]
     face = face_inverses.shape[2]
-    keep = jnp.repeat(block_pattern[0].astype(F32), width // block_pattern.shape[2], axis=1)
     vmem = pl.BlockSpec(memory_space=pltpu.VMEM)
+    anywhere = pl.BlockSpec(memory_space=pl.ANY)
     square = pltpu.VMEM((width, width), BF16)
     count = pltpu.SemaphoreType.DMA((width // CH,))
     merged, upward = pl.pallas_call(
@@ -428,9 +474,12 @@
             jax.ShapeDtypeStruct((width, width), BF16),
             jax.ShapeDtypeStruct((rhs, width), F32),
         ),
-        in_specs=[vmem] * 5,
-        out_specs=(vmem, vmem),
-        scratch_shapes=[square] * 6
+        in_specs=[anywhere, pl.BlockSpec(memory_space=pltpu.SMEM), anywhere, vmem, vmem],
+        out_specs=(anywhere, vmem),
+        scratch_shapes=[
+            square, square, pltpu.VMEM((3, face, face), F32), pltpu.SemaphoreType.DMA((16,)),
+        ]
+        + [square] * 6
         + [pltpu.VMEM((3, face, width), BF16), square, square]
         + [pltpu.VMEM((rhs, width), F32)] * 2
         + [pltpu.VMEM((rhs, width), BF16)] * 4
@@ -441,13 +490,25 @@
         + [pltpu.VMEM((boxes, boxes, rhs, CH), F32)] * 2
         + [pltpu.VMEM((boxes * rhs, CH), F32), pltpu.VMEM((boxes, rhs, width), F32)]
         + [count] * 8
-        + [pltpu.SemaphoreType.DMA((4,))] * 6
+        + [pltpu.SemaphoreType.DMA((8,))] * 6
         + [pltpu.SemaphoreType.DMA((2,))] * 2
         + [pltpu.SemaphoreType.DMA((boxes,))] * 8,
         compiler_params=pltpu.CompilerParams(
             collective_id=0, has_side_effects=True, vmem_limit_bytes=56 * 2**20
         ),
-    )(box_maps[0], keep, face_inverses[0], index_map, sources[0])
+    )(box_maps[0], block_pattern[0], face_inverses[0], index_map, sources[0])
+    merged, upward = pl.pallas_call(
+        hand_on,
+        out_shape=(
+            jax.ShapeDtypeStruct((width, width), BF16),
+            jax.ShapeDtypeStruct((rhs, width), F32),
+        ),
+        in_specs=[anywhere, anywhere],
+        out_specs=(anywhere, anywhere),
+        scratch_shapes=[
+            square, pltpu.VMEM((rhs, width), F32), pltpu.SemaphoreType.DMA((18,)),
+        ],
+    )(merged, upward)
     return (merged[None], upward[None])
 
 

time: 140 us -> 128 us (0.914)
  Pallas kernels: 134 us -> 127 us
  local copies, waits for them, and re-layouts: 4.45 us -> 0 us
    pallas_call x1, Pallas kernels: 134 us -> 125 us  [on_device(): pl.pallas_call(functools.partial(kernel, layers, coupling), out_shape=(ja...]
    unnamed x4 -> x0, local copies, waits for them, and re-layouts: 3.69 us -> none
    pallas_call x0 -> x1, Pallas kernels: none -> 2.42 us  [on_device(): pl.pallas_call(hand_on, out_shape=(jax.ShapeDtypeStruct((width, width), B...]
where the time goes in v4:
time: 128 us
  Pallas kernels  127 us (99%)
    pallas_call x1, Pallas kernels, on_device(): pl.pallas_call(functools.partial(kernel, layers, coupling), out_shape=(ja...  125 us

profile of v4, /device:TPU:33, one launch (start us, length us, event | category | flops | bytes accessed | tf_op | source)
XLA Modules:
  0.0 128.1 jit_solution(3104679534953435809)
XLA Ops:
  0.6 125.0 %shard_map.68 = (bf16[1024,1024]{1,0:T(8,128)(2,1)}, f32[2,1024]{1,0:T(2,128)}) custom-call(bf16[1024,1024]{1,0:T(8,128)(2,1)} %bitcast.6, s32[8,8]{1,0:T(8,128)} %bitcast.9, f32[7,256,256]{2,1,0:T(8,128)} %bitcast.7, s32[1,1024]{1,0:T(1,128)} %idx_ref.1, f32[2,1024]{1,0:T(2,128)} %bitcast.8), custom_call_target="tpu_custom_call" | custom-call | tf_op jit(solution)/shard_map/pallas_call | solution.py:471
  125.7 2.4 %shard_map.69 = (bf16[1024,1024]{1,0:T(8,128)(2,1)}, f32[2,1024]{1,0:T(2,128)}) custom-call(bf16[1024,1024]{1,0:T(8,128)(2,1)} %get-tuple-element.6.m_in, f32[2,1024]{1,0:T(2,128)} %get-tuple-element.7.u_in), custom_call_target="tpu_custom_call" | custom-call | tf_op jit(solution)/shard_map/pallas_call | solution.py:500

commit v5 on v4

--- a/solution.py
+++ b/solution.py
@@ -23,7 +23,7 @@
     leaf, part0, half1, part1, half2, part2, v_ref, pick, a_ref,
     d_ref, u_ref, send_d, send_u, down_buf, up_buf,
     phi, phi_in, psi, psi_in, res, res_in,
-    dcol, ucol, flat, part3, link_d, link_u, in_d, in_u, col16, last_in,
+    dcol, ucol, flat, part3, link_d, link_u, in_d, in_u, wide, last_in,
     s0, r0, s1, r1, s2, r2, q1, q2,
     phi_s, phi_r, psi_s, psi_r, res_s, res_r, one_s, one_r,
     ld_s, ld_r, lu_s, lu_r, bd_s, bu_s, f_s, f_r,
@@ -73,6 +73,11 @@
         load_map(k).start()
     for level in range(3):
         load_inverse(level).start()
+    @pl.loop(0, width // CH)
+    def _(step):
+        spot = lax.broadcasted_iota(jnp.int32, (CH, width), 0) + step * CH
+        pick[pl.ds(pl.multiple_of(step * CH, CH), CH), :] = (spot == idx_ref[...]).astype(F32).astype(BF16)
+
     for k in range(width // CH):
         load_map(k).wait()
         for j in range(width // CH):
@@ -110,11 +115,6 @@
 
     for k in range(width // CH):
         send(leaf, part0, k, s0, r0, sibling).start()
-
-    @pl.loop(0, width // CH)
-    def _(step):
-        spot = lax.broadcasted_iota(jnp.int32, (CH, width), 0) + step * CH
-        pick[rows(step), :] = (spot == idx_ref[...]).astype(F32).astype(BF16)
 
     def got(buf, k, ssem, rsem, mate):
         send(buf, buf, k, ssem, rsem, mate).wait_recv()
@@ -143,15 +143,20 @@
         mine, theirs = ORDER[step] + core, ORDER[step] + 1 - core
         got(part2, mine, s2, r2, cross)
         send(part2, part2, mine, q2, r2, sibling).start()
+        if step > 1:
+            merge(2, half2, part2, m_ref, mine)
+            permute(mine)
         got(part2, theirs, q2, r2, sibling)
         if step == 0:
             return
-        if step == 1:
-            make_v(2, half2, part2)
-        for other in (0, 1) if step == 1 else (step,):
-            for k in (ORDER[other], ORDER[other] + 1):
-                merge(2, half2, part2, m_ref, k)
-                permute(k)
+        if step > 1:
+            merge(2, half2, part2, m_ref, theirs)
+            permute(theirs)
+            return
+        make_v(2, half2, part2)
+        for k in (ORDER[0], ORDER[0] + 1, ORDER[1], ORDER[1] + 1):
+            merge(2, half2, part2, m_ref, k)
+            permute(k)
 
     for step, base in enumerate(ORDER):
         mine, theirs = base + core, base + 1 - core
@@ -286,25 +291,22 @@
                    group * depth + lax.rem(z + step, depth), box)
 
     def link_copy(link, buf, ssem, rsem, where, j):
-        return hop(link.at[:, :, pl.ds(j * CH, CH)], buf.at[box], ssem.at[j], rsem.at[box], where, j)
+        return hop(link.at[:, pl.ds(j * CH, CH)], buf.at[box], ssem.at[j], rsem.at[box], where, j)
 
     def gather_cols(link, buf, ssem, rsem, col):
         for j in range(boxes):
             hop(buf.at[j], buf.at[j], ssem.at[j], rsem.at[j], me, box).wait_recv()
-        total = buf[0]
+        total = buf[0].astype(F32)
         for j in range(1, boxes):
-            total = total + buf[j]
+            total = total + buf[j].astype(F32)
+        col[...] = total.astype(BF16)
+
+    def make_link(value, link, mine):
         for j in range(boxes):
-            col16[pl.ds(2 * j, 2), :] = total[j]
-        col[...] = col16[...].astype(BF16)
-
-    def unfold(value, link, mine):
-        flat[...] = value
-        for j in range(boxes):
-            part3[j] = flat[pl.ds(2 * j, 2), :]
-        if link is not None:
-            link[...] = part3[...]
-            link[box] += mine
+            wide[pl.ds(2 * j, 2), :] = mine
+        row = lax.broadcasted_iota(jnp.int32, wide.shape, 0) - 2 * box
+        own = jnp.logical_and(row >= 0, row < 2)
+        link[...] = (value + jnp.where(own, wide[...], 0.0)).astype(BF16)
 
     after = jnp.minimum(group + 1, blocks - 1) * depth + z
     before = jnp.maximum(group - 1, 0) * depth + z
@@ -326,7 +328,7 @@
 
         @pl.when(jnp.logical_not(bottom))
         def _():
-            unfold(dot(dcol[...], phi[...]), link_d, d_ref[...])
+            make_link(dot(dcol[...], phi[...]), link_d, d_ref[...])
             for j in range(boxes):
                 link_copy(link_d, in_d, ld_s, ld_r, after, j).start()
 
@@ -359,6 +361,8 @@
         def _():
             d_spread(1).wait_recv()
 
+    flat[...] = dot(dcol[...], res[...])
+
     @pl.when(first)
     def _():
         @pl.when(jnp.logical_not(bottom))
@@ -366,10 +370,11 @@
             gather_cols(link_u, in_u, lu_s, lu_r, ucol)
             spread(u_spread, True)
 
-        unfold(dot(dcol[...], res[...]) + dot(ucol[...], psi[...]), link_u, u_ref[...])
+        flat[...] += dot(ucol[...], psi[...])
 
         @pl.when(jnp.logical_not(top))
         def _():
+            make_link(flat[...], link_u, u_ref[...])
             for j in range(boxes):
                 link_copy(link_u, in_u, lu_s, lu_r, before, j).start()
 
@@ -379,7 +384,10 @@
         def _():
             u_spread(1).wait_recv()
 
-        unfold(dot(dcol[...], res[...]) + dot(ucol[...], psi[...]), None, None)
+        flat[...] += dot(ucol[...], psi[...])
+
+    for j in range(boxes):
+        part3[j] = flat[pl.ds(2 * j, 2), :].astype(BF16)
 
     def last_copy(step):
         mate = lax.rem(box + step, boxes)
@@ -387,10 +395,10 @@
 
     for step in range(1, boxes):
         last_copy(step).start()
-    total = u_ref[...] + part3[box]
+    total = u_ref[...] + part3[box].astype(F32)
     for step in range(1, boxes):
         last_copy(step).wait_recv()
-        total = total + last_in[step]
+        total = total + last_in[step].astype(F32)
     out_ref[...] = total
 
     store_map.wait()
@@ -486,9 +494,10 @@
         + [pltpu.VMEM((CH, width), BF16)] * 6
         + [pltpu.VMEM((boxes * rhs, CH), BF16)] * 2
         + [pltpu.VMEM((boxes * rhs, width), F32)]
-        + [pltpu.VMEM((boxes, rhs, width), F32)] * 3
-        + [pltpu.VMEM((boxes, boxes, rhs, CH), F32)] * 2
-        + [pltpu.VMEM((boxes * rhs, CH), F32), pltpu.VMEM((boxes, rhs, width), F32)]
+        + [pltpu.VMEM((boxes, rhs, width), BF16)]
+        + [pltpu.VMEM((boxes * rhs, width), BF16)] * 2
+        + [pltpu.VMEM((boxes, boxes * rhs, CH), BF16)] * 2
+        + [pltpu.VMEM((boxes * rhs, width), F32), pltpu.VMEM((boxes, rhs, width), BF16)]
         + [count] * 8
         + [pltpu.SemaphoreType.DMA((8,))] * 6
         + [pltpu.SemaphoreType.DMA((2,))] * 2

time: 128 us -> 128 us (level)
  no operation moved by 1% of the time
where the time goes in v5:
time: 128 us
  Pallas kernels  127 us (99%)
    pallas_call x1, Pallas kernels, on_device(): pl.pallas_call(functools.partial(kernel, layers, coupling), out_shape=(ja...  125 us

profile of v5, /device:TPU:33, one launch (start us, length us, event | category | flops | bytes accessed | tf_op | source)
XLA Modules:
  0.0 127.6 jit_solution(17975581568803520039)
XLA Ops:
  0.6 124.6 %shard_map.68 = (bf16[1024,1024]{1,0:T(8,128)(2,1)}, f32[2,1024]{1,0:T(2,128)}) custom-call(bf16[1024,1024]{1,0:T(8,128)(2,1)} %bitcast.6, s32[8,8]{1,0:T(8,128)} %bitcast.9, f32[7,256,256]{2,1,0:T(8,128)} %bitcast.7, s32[1,1024]{1,0:T(1,128)} %idx_ref.1, f32[2,1024]{1,0:T(2,128)} %bitcast.8), custom_call_target="tpu_custom_call" | custom-call | tf_op jit(solution)/shard_map/pallas_call | solution.py:479
  125.2 2.4 %shard_map.69 = (bf16[1024,1024]{1,0:T(8,128)(2,1)}, f32[2,1024]{1,0:T(2,128)}) custom-call(bf16[1024,1024]{1,0:T(8,128)(2,1)} %get-tuple-element.6.m_in, f32[2,1024]{1,0:T(2,128)} %get-tuple-element.7.u_in), custom_call_target="tpu_custom_call" | custom-call | tf_op jit(solution)/shard_map/pallas_call | solution.py:509
